TPU v7x, 32 devices: a whole 2x2x4 slice. The times are simulated.
32 devices in a mesh: section: 4 (over x, core), dp: 8 (over z, y).
Axes of the slice: x: 2, y: 2, z: 4, core: 2. Of those that a mesh axis runs over, the one named last changes fastest.
Arguments:
- token_ids: int32 [2, 16], P(None, 'dp'), may hold values from 0 to 8191
- target_ids: int32 [2, 16], P(None, 'dp'), may hold values from 0 to 8191
- table: bfloat16 [8192, 4608], P(('section', 'dp')), may hold values from -0.06629126 to 0.06629126
- norm_gain: bfloat16 [2, 4, 4608], P(None, 'section'), may hold values from 0.099609375 to 1.8984375
- w_in: bfloat16 [2, 4, 8, 4608], P(None, 'section'), may hold values from -0.09375 to 0.09375
- w_out: bfloat16 [2, 4, 8, 4608], P(None, 'section'), may hold values from -2 to 2
- final_gain: bfloat16 [4608], replicated, may hold values from 0.099609375 to 1.8984375
Outputs:
- token_loss: float32 [2, 16], P(None, 'dp')
- table_grad: bfloat16 [8192, 4608], P(('section', 'dp'))
All inputs are finite; a program needn't handle non-finite values.
Results may differ from a plain program's by a relative error of at most 0.013.
The roundings to bfloat16 on the way count: a program that leaves them out, or rounds other values in their place, can miss the bound.
Values may be sent and summed in bfloat16 or wider, within the bound.
A program may use at most 64 MiB of HBM per device.

v0:
```python
import math
import jax
import jax.numpy as jnp
from jax import lax
from jax.sharding import PartitionSpec as P

EPS = 1e-06
CAP = 30.0
GELU_C = 0.7978845608028654


def shifted(block, axis, distance):
    devices = range(lax.axis_size(axis))
    route = [((i - distance) % len(devices), i) for i in devices]
    return lax.ppermute(block, axis, route)


def from_root(block, axis, source):
    block = jnp.where(lax.axis_index(axis) == source, block, jnp.zeros_like(block))
    return lax.psum(block, axis)


def gelu_tanh(values):
    return 0.5 * values * (1.0 + jnp.tanh(GELU_C * (values + 0.044715 * values * values * values)))


def gelu_slope(values):
    inner = jnp.tanh(GELU_C * (values + 0.044715 * values * values * values))
    return 0.5 * (1.0 + inner) + 0.5 * values * (1.0 - inner * inner) * GELU_C * (
        1.0 + 3.0 * 0.044715 * values * values
    )


def normalize(rows_in):
    values = rows_in.astype(jnp.float32)
    scale = lax.rsqrt(jnp.mean(values * values, axis=-1, keepdims=True) + EPS)
    return (values * scale, scale)


def norm_back(normed, scale, grad):
    return scale * (grad - normed * jnp.mean(grad * normed, axis=-1, keepdims=True))


def layer_forward(rows_in, gain, first_proj, second_proj):
    normed, scale = normalize(rows_in)
    activated = (normed * gain.astype(jnp.float32)).astype(jnp.bfloat16)
    preact = lax.dot_general(
        activated, first_proj, (((1,), (1,)), ((), ())), preferred_element_type=jnp.float32
    )
    hidden = gelu_tanh(preact).astype(jnp.bfloat16)
    branch = jnp.dot(hidden, second_proj, preferred_element_type=jnp.float32)
    return (rows_in.astype(jnp.float32) + branch).astype(jnp.bfloat16)


def layer_backward(rows_in, gain, first_proj, second_proj, grad_out):
    normed, scale = normalize(rows_in)
    gain_float = gain.astype(jnp.float32)
    activated = (normed * gain_float).astype(jnp.bfloat16)
    preact = lax.dot_general(
        activated, first_proj, (((1,), (1,)), ((), ())), preferred_element_type=jnp.float32
    )
    hidden_grad = lax.dot_general(
        grad_out, second_proj, (((1,), (1,)), ((), ())), preferred_element_type=jnp.float32
    )
    preact_grad = (hidden_grad * gelu_slope(preact)).astype(jnp.bfloat16)
    act_grad = jnp.dot(preact_grad, first_proj, preferred_element_type=jnp.float32)
    return (grad_out.astype(jnp.float32) + norm_back(normed, scale, act_grad * gain_float)).astype(
        jnp.bfloat16
    )


def per_device(token_ids, target_ids, table, norm_gain, w_in, w_out, final_gain):
    sections = lax.axis_size("section")
    section_index = lax.axis_index("section")
    replicas = lax.axis_size("dp")
    replica_index = lax.axis_index("dp")
    batches, width = token_ids.shape
    rows_dev, dim = table.shape
    embed_scale = math.sqrt(dim)
    offset = (section_index * replicas + replica_index) * rows_dev
    columns = jnp.arange(rows_dev, dtype=jnp.int32)
    final_scale = final_gain.astype(jnp.float32)
    ids = lax.all_gather(jnp.concatenate([token_ids, target_ids], 0), "dp", axis=1, tiled=True)
    gains = lax.all_gather(norm_gain, "section", axis=1, tiled=True).reshape(-1, dim)
    first = lax.all_gather(w_in, "section", axis=1, tiled=True).reshape(2 * sections, -1, dim)
    second = lax.all_gather(w_out, "section", axis=1, tiled=True).reshape(2 * sections, -1, dim)
    all_inputs, all_targets = (ids[:batches], ids[batches:])
    wide = all_inputs.shape[1]
    token_count = batches * wide
    chosen = ((all_inputs.reshape(token_count) - offset)[:, None] == columns[None, :]).astype(
        jnp.bfloat16
    )
    looked = jnp.dot(chosen, table, preferred_element_type=jnp.float32).astype(jnp.bfloat16)
    looked = lax.psum(looked, ("section", "dp")).astype(jnp.float32)
    rows = (looked * embed_scale).astype(jnp.bfloat16)

    def forward(rows, weights):
        return (layer_forward(rows, *weights), rows)

    rows, inputs = lax.scan(forward, rows, (gains, first, second))
    normed, scale = normalize(rows)
    head_input = (normed * final_scale).astype(jnp.bfloat16)
    scores = lax.dot_general(
        head_input, table, (((1,), (1,)), ((), ())), preferred_element_type=jnp.float32
    )
    squash = jnp.tanh(scores / CAP)
    capped = CAP * squash
    powers = jnp.exp(capped)
    goal_local = all_targets.reshape(token_count) - offset
    target_mask = goal_local[:, None] == columns[None, :]
    stats = lax.psum(
        jnp.stack(
            [
                jnp.sum(powers, axis=1),
                jnp.sum(jnp.where(target_mask, capped, jnp.float32(0.0)), axis=1),
            ]
        ),
        ("section", "dp"),
    )
    exp_total, target_score = (stats[0], stats[1])
    loss_all = (jnp.log(exp_total) - target_score).reshape(batches, wide)
    token_loss = lax.dynamic_slice_in_dim(loss_all, replica_index * width, width, 1)
    score_grad = (
        (powers / exp_total[:, None] - target_mask.astype(jnp.float32)) * (1.0 - squash * squash)
    ).astype(jnp.bfloat16)
    partial_value = jnp.dot(score_grad, table, preferred_element_type=jnp.float32)
    head_in_grad = lax.psum(partial_value, ("section", "dp"))
    grad = norm_back(normed, scale, head_in_grad * final_scale).astype(jnp.bfloat16)

    def backward(grad, saved):
        return (layer_backward(*saved, grad), None)

    grad, _ = lax.scan(backward, grad, (inputs, gains, first, second), reverse=True)
    head_grad = lax.dot_general(
        score_grad, head_input, (((0,), (0,)), ((), ())), preferred_element_type=jnp.float32
    )
    embed_grad = (
        lax.dot_general(chosen, grad, (((0,), (0,)), ((), ())), preferred_element_type=jnp.float32)
        * embed_scale
    )
    return (token_loss, (head_grad + embed_grad).astype(jnp.bfloat16))


def solution(mesh):
    return jax.shard_map(
        per_device,
        mesh=mesh,
        in_specs=(
            P(None, "dp"),
            P(None, "dp"),
            P(("section", "dp"), None),
            P(None, "section", None),
            P(None, "section", None, None),
            P(None, "section", None, None),
            P(),
        ),
        out_specs=(P(None, "dp"), P(("section", "dp"), None)),
        check_vma=False,
    )
```

profile of v0, /device:TPU:0, one launch (start us, length us, event | category | flops | bytes accessed | tf_op | source)
XLA Modules:
  0.0 419.9 jit_solution(2897440791546498494)
XLA Ops:
  8.2 22.3 %all-gather = s32[8,2,4]{2,1,0:T(2,128)S(1)} all-gather(s32[1,2,4]{2,1,0:T(2,128)S(1)} %bitcast.102), channel_id=1, replica_groups=mesh['section'=4,'dp'=8] {'dp'}, dimensions={0}, use_global_device_ids=true | all-gather | bytes 288 | tf_op jit(solution)/shard_map/all_gather | solution.py:83
  30.6 1.2 convolution_convert_fusion
  32.1 5.3 %all_gather.13 = bf16[2,4,4608]{2,0,1:T(2,128)(2,1)S(1)} all-gather(bf16[2,1,4608]{2,0,1:T(2,128)(2,1)S(1)} %copy-done.3), channel_id=1, replica_groups=mesh['section'=4,'dp'=8] {'section'}, dimensions={1}, use_global_device_ids=true | all-gather | bytes 92160 | tf_op jit(solution)/shard_map/all_gather | solution.py:84
  38.0 8.2 %all_gather.14 = bf16[2,4,8,4608]{3,2,1,0:T(8,128)(2,1)} all-gather(bf16[2,1,8,4608]{3,2,1,0:T(8,128)(2,1)S(1)} %copy-done.1), channel_id=1, replica_groups=mesh['section'=4,'dp'=8] {'section'}, dimensions={1}, use_global_device_ids=true | all-gather | bytes 737280 | tf_op jit(solution)/shard_map/all_gather | solution.py:85
  46.2 8.1 %all_gather.15 = bf16[2,4,8,4608]{3,2,1,0:T(8,128)(2,1)} all-gather(bf16[2,1,8,4608]{3,2,1,0:T(8,128)(2,1)S(1)} %copy-done.2), channel_id=1, replica_groups=mesh['section'=4,'dp'=8] {'section'}, dimensions={1}, use_global_device_ids=true | all-gather | bytes 737280 | tf_op jit(solution)/shard_map/all_gather | solution.py:86
  54.3 100.7 %all-reduce.3.cloned.1.call-done = bf16[32,4608]{1,0:T(8,128)(2,1)} async-done(((bf16[32,4608]{1,0:T(8,128)(2,1)}), bf16[32,4608]{1,0:T(8,128)(2,1)}) %all-reduce.3.cloned.1.call-update) | async-done | bytes 294928 | tf_op jit(solution)/shard_map/psum | solution.py:94
  156.0 28.2 %while.26 = (s32[]{:T(128)}, bf16[32,4608]{1,0:T(8,128)(2,1)S(1)}, bf16[8,32,4608]{2,1,0:T(8,128)(2,1)}, bf16[8,4608]{1,0:T(8,128)(2,1)}, bf16[8,8,4608]{2,1,0:T...) while((s32[]{:T(128)}, bf16[32,4608]{1,0:T(8,128)(2,1)S(1)}, bf16[8,32,4608]{2,1,0:T(8,128)(2,1)}, ...), condition=%wide.region_3.4_spmd, body=%wide.region_1.3_spmd.sunk | while | flops 6200098 | bytes 2556893 | solution.py:100
  157.9 1.6 fusion.132
  161.5 1.6 fusion.132
  165.0 1.6 fusion.132
  168.5 1.6 fusion.132
  172.1 1.6 fusion.132
  175.6 1.6 fusion.132
  179.1 1.6 fusion.132
  182.7 1.6 fusion.132
  185.4 41.2 %psum.22 = f32[2,32]{1,0:T(2,128)S(1)} all-reduce(f32[2,32]{1,0:T(2,128)S(1)} %pad_maximum_fusion), channel_id=1, replica_groups=mesh['section'=4,'dp'=8] {'section','dp'}, use_global_device_ids=true, to_apply=%region_7.8 | all-reduce | flops 64 | bytes 512 | tf_op jit(solution)/shard_map/psum | solution.py:111
  226.7 1.4 fusion.107
  228.8 3.0 fusion.102
  231.8 123.7 %all-reduce.5.cloned.1.call-done = f32[32,4608]{1,0:T(8,128)} async-done(((f32[32,4608]{1,0:T(8,128)}), f32[32,4608]{1,0:T(8,128)}) %all-reduce.5.cloned.1.call-update) | async-done | bytes 589840 | tf_op jit(solution)/shard_map/psum | solution.py:127
  355.5 1.3 fusion.97
  356.8 1.2 fusion.100
  358.0 50.4 %while.27 = (s32[]{:T(128)}, bf16[32,4608]{1,0:T(8,128)(2,1)S(1)}, bf16[8,32,4608]{2,1,0:T(8,128)(2,1)}, bf16[8,8,4608]{2,1,0:T(8,128)(2,1)}, bf16[8,4608]{1,0:T...) while((s32[]{:T(128)}, bf16[32,4608]{1,0:T(8,128)(2,1)S(1)}, ...), condition=%wide.region_13.14_spmd, body=%wide.region_10.13_spmd.sunk | while | flops 10036515 | bytes 3535725 | solution.py:133
  358.0 1.1 fusion.137
  360.1 1.2 fusion.138
  361.4 1.7 fusion.139
  363.1 1.2 fusion.140
  366.4 1.2 fusion.138
  367.7 1.7 fusion.139
  369.4 1.2 fusion.140
  372.7 1.2 fusion.138
  374.0 1.7 fusion.139
  375.7 1.2 fusion.140
  379.0 1.2 fusion.138
  380.3 1.7 fusion.139
  382.0 1.2 fusion.140
  385.3 1.2 fusion.138
  386.6 1.7 fusion.139
  388.3 1.2 fusion.140
  391.6 1.2 fusion.138
  392.9 1.7 fusion.139
  394.6 1.2 fusion.140
  397.9 1.2 fusion.138
  399.1 1.7 fusion.139
  400.9 1.2 fusion.140
  404.2 1.2 fusion.138
  405.4 1.7 fusion.139
  407.2 1.2 fusion.140
  408.4 4.6 %fusion.91 = bf16[256,4608]{1,0:T(8,128)(2,1)} fusion(f32[256,4608]{1,0:T(8,128)} %fusion.102, bf16[32,4608]{1,0:T(8,128)(2,1)S(1)} %get-tuple-element.159, s32[32]{0:T(128)S(1)} %sub.70), kind=kOutput, calls=%fused_computation.92 | convolution fusion | flops 79044608 | bytes 7372928 | tf_op jit(solution)/shard_map/dot_general | solution.py:138
  (104 shorter events, 35.8 us)
Async XLA Ops:
  7.2 23.5 %copy-start = (bf16[256,4608]{1,0:T(8,128)(2,1)S(1)}, bf16[256,4608]{1,0:T(8,128)(2,1)}, u32[]{:S(2)}) copy-start(bf16[256,4608]{1,0:T(8,128)(2,1)} %param.13) | copy-start | bytes 7077892
  7.2 24.9 %copy-start.4 = (bf16[4608]{0:T(1024)(128)(2,1)S(1)}, bf16[4608]{0:T(1024)(128)(2,1)}, u32[]{:S(2)}) copy-start(bf16[4608]{0:T(1024)(128)(2,1)} %param.17) | copy-start | bytes 27652
  7.2 24.9 %copy-start.3 = (bf16[2,1,4608]{2,0,1:T(2,128)(2,1)S(1)}, bf16[2,1,4608]{2,0,1:T(2,128)(2,1)}, u32[]{:S(2)}) copy-start(bf16[2,1,4608]{2,0,1:T(2,128)(2,1)} %param.14) | copy-start | bytes 55300
  7.2 30.8 %copy-start.1 = (bf16[2,1,8,4608]{3,2,1,0:T(8,128)(2,1)S(1)}, bf16[2,1,8,4608]{3,2,1,0:T(8,128)(2,1)}, u32[]{:S(2)}) copy-start(bf16[2,1,8,4608]{3,2,1,0:T(8,128)(2,1)} %param.15) | copy-start | bytes 442372
  7.2 39.0 %copy-start.2 = (bf16[2,1,8,4608]{3,2,1,0:T(8,128)(2,1)S(1)}, bf16[2,1,8,4608]{3,2,1,0:T(8,128)(2,1)}, u32[]{:S(2)}) copy-start(bf16[2,1,8,4608]{3,2,1,0:T(8,128)(2,1)} %param.16) | copy-start | bytes 442372
  7.2 147.8 %all-reduce.3.cloned.1.call-start = ((), (), s32[]{:S(2)}) async-start(), calls=%async_computation | async-start | bytes 589824 | tf_op jit(solution)/shard_map/psum | solution.py:94
  31.9 323.5 %all-reduce.5.cloned.1.call-start = ((), (), s32[]{:S(2)}) async-start(), calls=%async_computation.1 | async-start | bytes 1179648 | tf_op jit(solution)/shard_map/psum | solution.py:127
Sparse Core Ops, SparseCore 0:
  32.0 122.9 all-reduce.2
  228.3 127.1 all-reduce.4
where the time goes:
time: 422 us; the launch traced here: 420 us
  waiting for transfers between devices  224 us (53%)
  blocking collectives  85 us (20%)
  matrix products  47.9 us (11%)
  other arithmetic  40 us (9%)
  between operations  14.1 us (3%)
  local copies, waits for them, and re-layouts  7.85 us (2%)
    psum x1, waiting for transfers between devices, per_device(): head_in_grad = lax.psum(partial_value, ('section', 'dp'))  124 us
    psum x1, waiting for transfers between devices, per_device(): looked = lax.psum(looked, ('section', 'dp')).astype(jnp.float32)  101 us
    psum x1, blocking collectives, per_device(): lax.psum(jnp.stack([jnp.sum(powers, axis=1), jnp.sum(jnp.where(target_mas...  41.2 us
    all_gather x1, blocking collectives, per_device(): lax.all_gather(jnp.concatenate([token_ids, target_ids], 0), 'dp', axis=1,...  22.3 us
    dot_general x8, matrix products, layer_backward(): jnp.dot(preact_grad, first_proj, preferred_element_type=jnp.float32)  14 us
    dot_general x8, matrix products, layer_forward(): branch = jnp.dot(hidden, second_proj, preferred_element_type=jnp.float32)  12.8 us
    reduce_sum x17, other arithmetic, normalize(): scale = lax.rsqrt(jnp.mean(values * values, axis=-1, keepdims=True) + EPS)  10.7 us
    dot_general x8, matrix products, layer_backward(): lax.dot_general(activated, first_proj, (((1,), (1,)), ((), ())), preferre...  9.88 us
  transfers between devices with their start and end apart: 2, of which 2 were waited for; matrix products, arithmetic and copies ran while one was open for 1% of the time, Pallas kernels for 0%

commit v1 on v0

--- a/solution.py
+++ b/solution.py
@@ -108,15 +108,11 @@
     powers = jnp.exp(capped)
     goal_local = all_targets.reshape(token_count) - offset
     target_mask = goal_local[:, None] == columns[None, :]
-    stats = lax.psum(
-        jnp.stack(
-            [
-                jnp.sum(powers, axis=1),
-                jnp.sum(jnp.where(target_mask, capped, jnp.float32(0.0)), axis=1),
-            ]
-        ),
-        ("section", "dp"),
+    block_2 = jnp.stack(
+        [jnp.sum(powers, axis=1), jnp.sum(jnp.where(target_mask, capped, jnp.float32(0.0)), axis=1)]
     )
+    shards = lax.all_gather(block_2, ("section", "dp"))
+    stats = jnp.sum(shards, axis=0)
     exp_total, target_score = (stats[0], stats[1])
     loss_all = (jnp.log(exp_total) - target_score).reshape(batches, wide)
     token_loss = lax.dynamic_slice_in_dim(loss_all, replica_index * width, width, 1)

time: 422 us -> 445 us (1.055)
  blocking collectives: 85 us -> 111 us
    all_gather x0 -> x1, blocking collectives: none -> 67.1 us  [per_device(): shards = lax.all_gather(block_2, ('section', 'dp'))]
    psum x1 -> x0, blocking collectives: 41.2 us -> none  [per_device(): lax.psum(jnp.stack([jnp.sum(powers, axis=1), jnp.sum(jnp.where(target_mas...]
where the time goes in v1:
time: 445 us; the launch traced here: 442 us
  waiting for transfers between devices  221 us (50%)
  blocking collectives  111 us (25%)
  matrix products  47.9 us (11%)
  other arithmetic  40.1 us (9%)
  between operations  14.1 us (3%)
  local copies, waits for them, and re-layouts  7.85 us (2%)
    psum x1, waiting for transfers between devices, per_device(): head_in_grad = lax.psum(partial_value, ('section', 'dp'))  120 us
    psum x1, waiting for transfers between devices, per_device(): looked = lax.psum(looked, ('section', 'dp')).astype(jnp.float32)  101 us
    all_gather x1, blocking collectives, per_device(): shards = lax.all_gather(block_2, ('section', 'dp'))  67.1 us
    all_gather x1, blocking collectives, per_device(): lax.all_gather(jnp.concatenate([token_ids, target_ids], 0), 'dp', axis=1,...  22.3 us
    dot_general x8, matrix products, layer_backward(): jnp.dot(preact_grad, first_proj, preferred_element_type=jnp.float32)  14 us
    dot_general x8, matrix products, layer_forward(): branch = jnp.dot(hidden, second_proj, preferred_element_type=jnp.float32)  12.8 us
    reduce_sum x17, other arithmetic, normalize(): scale = lax.rsqrt(jnp.mean(values * values, axis=-1, keepdims=True) + EPS)  10.7 us
    dot_general x8, matrix products, layer_backward(): lax.dot_general(activated, first_proj, (((1,), (1,)), ((), ())), preferre...  9.88 us
  transfers between devices with their start and end apart: 2, of which 2 were waited for; matrix products, arithmetic and copies ran while one was open for 1% of the time, Pallas kernels for 0%

profile of v1, /device:TPU:0, one launch (start us, length us, event | category | flops | bytes accessed | tf_op | source)
XLA Modules:
  0.0 442.3 jit_solution(11885547503362035623)
XLA Ops:
  8.2 22.3 %all-gather.1 = s32[8,2,4]{2,1,0:T(2,128)S(1)} all-gather(s32[1,2,4]{2,1,0:T(2,128)S(1)} %bitcast.104), channel_id=1, replica_groups=mesh['section'=4,'dp'=8] {'dp'}, dimensions={0}, use_global_device_ids=true | all-gather | bytes 288 | tf_op jit(solution)/shard_map/all_gather | solution.py:83
  30.6 1.2 convolution_convert_fusion
  32.1 5.3 %all_gather.19 = bf16[2,4,4608]{2,0,1:T(2,128)(2,1)S(1)} all-gather(bf16[2,1,4608]{2,0,1:T(2,128)(2,1)S(1)} %copy-done.3), channel_id=1, replica_groups=mesh['section'=4,'dp'=8] {'section'}, dimensions={1}, use_global_device_ids=true | all-gather | bytes 92160 | tf_op jit(solution)/shard_map/all_gather | solution.py:84
  38.0 8.2 %all_gather.20 = bf16[2,4,8,4608]{3,2,1,0:T(8,128)(2,1)} all-gather(bf16[2,1,8,4608]{3,2,1,0:T(8,128)(2,1)S(1)} %copy-done.1), channel_id=1, replica_groups=mesh['section'=4,'dp'=8] {'section'}, dimensions={1}, use_global_device_ids=true | all-gather | bytes 737280 | tf_op jit(solution)/shard_map/all_gather | solution.py:85
  46.2 8.1 %all_gather.21 = bf16[2,4,8,4608]{3,2,1,0:T(8,128)(2,1)} all-gather(bf16[2,1,8,4608]{3,2,1,0:T(8,128)(2,1)S(1)} %copy-done.2), channel_id=1, replica_groups=mesh['section'=4,'dp'=8] {'section'}, dimensions={1}, use_global_device_ids=true | all-gather | bytes 737280 | tf_op jit(solution)/shard_map/all_gather | solution.py:86
  54.3 100.7 %all-reduce.3.cloned.1.call-done = bf16[32,4608]{1,0:T(8,128)(2,1)} async-done(((bf16[32,4608]{1,0:T(8,128)(2,1)}), bf16[32,4608]{1,0:T(8,128)(2,1)}) %all-reduce.3.cloned.1.call-update) | async-done | bytes 294928 | tf_op jit(solution)/shard_map/psum | solution.py:94
  156.0 28.2 %while.26 = (s32[]{:T(128)}, bf16[32,4608]{1,0:T(8,128)(2,1)S(1)}, bf16[8,32,4608]{2,1,0:T(8,128)(2,1)}, bf16[8,4608]{1,0:T(8,128)(2,1)}, bf16[8,8,4608]{2,1,0:T...) while((s32[]{:T(128)}, bf16[32,4608]{1,0:T(8,128)(2,1)S(1)}, bf16[8,32,4608]{2,1,0:T(8,128)(2,1)}, ...), condition=%wide.region_3.4_spmd, body=%wide.region_1.3_spmd.sunk | while | flops 6200098 | bytes 2556893 | solution.py:100
  157.9 1.6 fusion.132
  161.5 1.6 fusion.132
  165.0 1.6 fusion.132
  168.5 1.6 fusion.132
  172.1 1.6 fusion.132
  175.6 1.6 fusion.132
  179.1 1.6 fusion.132
  182.7 1.6 fusion.132
  185.4 67.1 %all-gather.2 = f32[32,2,32]{2,1,0:T(2,128)S(1)} all-gather(f32[1,2,32]{2,1,0:T(2,128)S(1)} %maximum_bitcast_fusion), channel_id=2, replica_groups=mesh['section'=4,'dp'=8] {'section','dp'}, dimensions={0}, use_global_device_ids=true | all-gather | bytes 8448 | tf_op jit(solution)/shard_map/all_gather | solution.py:114
  252.7 1.4 fusion.107
  254.8 3.0 fusion.102
  257.8 120.1 %all-reduce.5.cloned.1.call-done = f32[32,4608]{1,0:T(8,128)} async-done(((f32[32,4608]{1,0:T(8,128)}), f32[32,4608]{1,0:T(8,128)}) %all-reduce.5.cloned.1.call-update) | async-done | bytes 589840 | tf_op jit(solution)/shard_map/psum | solution.py:123
  377.9 1.3 fusion.97
  379.2 1.2 fusion.100
  380.5 50.4 %while.27 = (s32[]{:T(128)}, bf16[32,4608]{1,0:T(8,128)(2,1)S(1)}, bf16[8,32,4608]{2,1,0:T(8,128)(2,1)}, bf16[8,8,4608]{2,1,0:T(8,128)(2,1)}, bf16[8,4608]{1,0:T...) while((s32[]{:T(128)}, bf16[32,4608]{1,0:T(8,128)(2,1)S(1)}, ...), condition=%wide.region_13.14_spmd, body=%wide.region_10.13_spmd.sunk | while | flops 10036515 | bytes 3535725 | solution.py:129
  382.6 1.2 fusion.138
  383.8 1.7 fusion.139
  385.6 1.2 fusion.140
  388.9 1.2 fusion.138
  390.1 1.7 fusion.139
  391.9 1.2 fusion.140
  395.2 1.2 fusion.138
  396.4 1.7 fusion.139
  398.2 1.2 fusion.140
  401.5 1.2 fusion.138
  402.7 1.7 fusion.139
  404.5 1.2 fusion.140
  405.7 1.1 fusion.137
  407.8 1.2 fusion.138
  409.0 1.7 fusion.139
  410.8 1.2 fusion.140
  414.1 1.2 fusion.138
  415.3 1.7 fusion.139
  417.1 1.2 fusion.140
  420.4 1.2 fusion.138
  421.6 1.7 fusion.139
  423.4 1.2 fusion.140
  426.7 1.2 fusion.138
  427.9 1.7 fusion.139
  429.7 1.2 fusion.140
  430.8 4.6 %fusion.91 = bf16[256,4608]{1,0:T(8,128)(2,1)} fusion(f32[256,4608]{1,0:T(8,128)} %fusion.102, bf16[32,4608]{1,0:T(8,128)(2,1)S(1)} %get-tuple-element.159, s32[32]{0:T(128)S(1)} %sub.70), kind=kOutput, calls=%fused_computation.92 | convolution fusion | flops 79044608 | bytes 7372928 | tf_op jit(solution)/shard_map/dot_general | solution.py:134
  (105 shorter events, 35.8 us)
Async XLA Ops:
  7.2 23.5 %copy-start = (bf16[256,4608]{1,0:T(8,128)(2,1)S(1)}, bf16[256,4608]{1,0:T(8,128)(2,1)}, u32[]{:S(2)}) copy-start(bf16[256,4608]{1,0:T(8,128)(2,1)} %param.13) | copy-start | bytes 7077892
  7.2 24.9 %copy-start.4 = (bf16[4608]{0:T(1024)(128)(2,1)S(1)}, bf16[4608]{0:T(1024)(128)(2,1)}, u32[]{:S(2)}) copy-start(bf16[4608]{0:T(1024)(128)(2,1)} %param.17) | copy-start | bytes 27652
  7.2 24.9 %copy-start.3 = (bf16[2,1,4608]{2,0,1:T(2,128)(2,1)S(1)}, bf16[2,1,4608]{2,0,1:T(2,128)(2,1)}, u32[]{:S(2)}) copy-start(bf16[2,1,4608]{2,0,1:T(2,128)(2,1)} %param.14) | copy-start | bytes 55300
  7.2 30.8 %copy-start.1 = (bf16[2,1,8,4608]{3,2,1,0:T(8,128)(2,1)S(1)}, bf16[2,1,8,4608]{3,2,1,0:T(8,128)(2,1)}, u32[]{:S(2)}) copy-start(bf16[2,1,8,4608]{3,2,1,0:T(8,128)(2,1)} %param.15) | copy-start | bytes 442372
  7.2 39.0 %copy-start.2 = (bf16[2,1,8,4608]{3,2,1,0:T(8,128)(2,1)S(1)}, bf16[2,1,8,4608]{3,2,1,0:T(8,128)(2,1)}, u32[]{:S(2)}) copy-start(bf16[2,1,8,4608]{3,2,1,0:T(8,128)(2,1)} %param.16) | copy-start | bytes 442372
  7.2 147.8 %all-reduce.3.cloned.1.call-start = ((), (), s32[]{:S(2)}) async-start(), calls=%async_computation | async-start | bytes 589824 | tf_op jit(solution)/shard_map/psum | solution.py:94
  31.9 346.0 %all-reduce.5.cloned.1.call-start = ((), (), s32[]{:S(2)}) async-start(), calls=%async_computation.1 | async-start | bytes 1179648 | tf_op jit(solution)/shard_map/psum | solution.py:123
Sparse Core Ops, SparseCore 0:
  32.0 122.9 all-reduce.2
  254.2 123.6 all-reduce.4
